TPU v7x, 256 devices: a whole 4x4x8 slice. The times are simulated.
256 devices in a mesh: dp: 16 (over y, z_hi, core), mp: 16 (over x, z_lo).
Axes of the slice: x: 4, y: 4, z: 8 (z_hi: 2, z_lo: 4; z = z_hi * 4 + z_lo), core: 2. Of those that a mesh axis runs over, the one named last changes fastest.
Arguments:
- skip_stream_arriving: float32 [4096, 2304], P('dp', 'mp'), may hold values from -170 to 170
- chosen_specialists: int32 [4096, 2], P('dp'), may hold values from 0 to 3, all different within a row; in each aligned block of 256 rows (0 to 255, 256 to 511, ...) at most 160 rows name the same one
- sequence_piece_tallies: int32 [16, 4], P('dp'), may hold values from 1 to 128, 256 in all within a row
- premix_rmsnorm_gain: float32 [2304], P('mp'), may hold values from 0.1 to 1.9
- dispatcher_weights: bfloat16 [2304, 4], replicated, may hold values from -0.125 to 0.125
- specialist_switch_weights: bfloat16 [4, 2304, 5760], P(None, 'dp', 'mp'), may hold values from -0.125 to 0.125
- specialist_expand_weights: bfloat16 [4, 2304, 5760], P(None, 'dp', 'mp'), may hold values from -0.125 to 0.125
- specialist_contract_weights: bfloat16 [4, 5760, 2304], P(None, 'mp', 'dp'), may hold values from -0.109375 to 0.109375
- terminal_rmsnorm_gain: float32 [2304], replicated, may hold values from 0.1 to 1.9
- lexicon_projector_weights: bfloat16 [2304, 131072], P(None, ('dp', 'mp')), may hold values from -12 to 12
- softness_per_sequence: float32 [64], replicated, may hold values from 0.02 to 1.5
Outputs:
- new_hidden: float32 [4096, 2304], P('dp', 'mp')
- logprobs: float32 [64, 131072], P(None, ('dp', 'mp'))
Inputs may be any that keep to these rules, and one draw needn't show every extreme that they name: `chosen_specialists`: in the 256 rows of each data group no expert is named by more than 160 rows, a bound that some block reaches. `sequence_piece_tallies`: each row sums to 256; its largest entry is 128.
All inputs are finite; a program needn't handle non-finite values.
Results may differ from a plain program's by a relative error of at most 0.0014.
Values may be sent and summed in bfloat16 or wider, within the bound.
A program may use at most 128 MiB of HBM per device.

v0:
```python
import math

import jax
import jax.numpy as jnp
from jax import lax
from jax.sharding import PartitionSpec as P

EMBED_DIMENSION = 2304
CAP = 160


branch_scale = 1.4 / math.sqrt(40.0)
epsilon = 1e-05


def slot_tables(routes_grp, expert, capacity):
    count = routes_grp.shape[0]
    hit = jnp.any(routes_grp == expert, axis=1)
    second = (routes_grp[:, 1] == expert).astype(jnp.int32)
    order = jnp.cumsum(hit.astype(jnp.int32), dtype=jnp.int32) - 1
    target = jnp.where(hit, order, capacity)
    tokens = jnp.arange(count, dtype=jnp.int32)
    slot_rows = jnp.zeros((capacity,), jnp.int32).at[target].set(tokens, mode="drop")
    live = jnp.zeros((capacity,), jnp.float32).at[target].set(1.0, mode="drop")
    which = jnp.zeros((capacity,), jnp.int32).at[target].set(second, mode="drop")
    return (slot_rows, live, which)


def body(
    skip_stream_arriving,
    chosen_specialists,
    sequence_piece_tallies,
    premix_rmsnorm_gain,
    dispatcher_weights,
    specialist_switch_weights,
    specialist_expand_weights,
    specialist_contract_weights,
    terminal_rmsnorm_gain,
    lexicon_projector_weights,
    softness_per_sequence,
):
    tok_rows = skip_stream_arriving.shape[0]
    local_width = skip_stream_arriving.shape[1]
    experts = specialist_switch_weights.shape[0]
    unit_cols = specialist_switch_weights.shape[2]
    squares = lax.psum(jnp.sum(skip_stream_arriving * skip_stream_arriving, axis=1), "mp")
    normed_local = (
        skip_stream_arriving
        * lax.rsqrt(squares / EMBED_DIMENSION + epsilon)[:, None]
        * premix_rmsnorm_gain
    ).astype(jnp.bfloat16)
    features = lax.all_gather(normed_local, "mp", axis=1, tiled=True)
    router = jnp.dot(features, dispatcher_weights, preferred_element_type=jnp.float32)
    mixing = jax.nn.softmax(jnp.take_along_axis(router, chosen_specialists, axis=1), axis=1)
    tables = [slot_tables(chosen_specialists, expert, CAP) for expert in range(experts)]
    inputs = jnp.stack([features[table[0]] for table in tables])
    scales = jnp.stack([mixing[table[0], table[2]] * table[1] for table in tables])
    pieces_out = []
    for expert in range(experts):
        rows_in = inputs[expert]

        def add_pair(carry, pieces, start, rows_in=rows_in):
            return (
                jnp.dot(rows_in, pieces[0], preferred_element_type=jnp.float32),
                jnp.dot(rows_in, pieces[1], preferred_element_type=jnp.float32),
            )

        empty = jnp.zeros((CAP, unit_cols), jnp.float32)
        gate, up_part = add_pair(
            (empty, empty),
            (
                lax.all_gather(specialist_switch_weights[expert], "dp", axis=0, tiled=True),
                lax.all_gather(specialist_expand_weights[expert], "dp", axis=0, tiled=True),
            ),
            jnp.int32(0),
        )
        act = (jax.nn.silu(gate) * up_part).astype(jnp.bfloat16)

        def project(piece, start, act=act):
            return jnp.dot(act, piece, preferred_element_type=jnp.float32)

        pieces_out.append(
            project(
                lax.all_gather(specialist_contract_weights[expert], "dp", axis=1, tiled=True),
                jnp.int32(0),
            )
        )
    outputs = jnp.stack(pieces_out)
    combined = jnp.zeros((tok_rows, EMBED_DIMENSION), jnp.float32)
    for expert in range(experts):
        combined = combined.at[tables[expert][0]].add(outputs[expert] * scales[expert][:, None])
    branch = lax.psum_scatter(
        combined.astype(jnp.bfloat16), "mp", scatter_dimension=1, tiled=True
    ).astype(jnp.float32)
    new_hidden = skip_stream_arriving + branch_scale * branch
    ends_index = jnp.cumsum(sequence_piece_tallies[0], dtype=jnp.int32) - 1
    end_local = new_hidden[ends_index]
    groups = lax.axis_size("dp")
    columns_count = lax.axis_size("mp")
    req_count = ends_index.shape[0]
    end_squares = lax.psum(jnp.sum(end_local * end_local, axis=1), "mp")
    gain_local = lax.dynamic_slice_in_dim(
        terminal_rmsnorm_gain, lax.axis_index("mp") * local_width, local_width
    )
    end_normed = (
        end_local * lax.rsqrt(end_squares / EMBED_DIMENSION + epsilon)[:, None] * gain_local
    ).astype(jnp.bfloat16)
    shaped = lax.all_gather(end_normed[None], ("dp", "mp"), axis=0, tiled=True).reshape(
        groups, columns_count, req_count, local_width
    )
    lexicon_projector_feed = shaped.transpose(0, 2, 1, 3).reshape(
        groups * req_count, columns_count * local_width
    )
    lexicon_logit_values = jnp.dot(
        lexicon_projector_feed, lexicon_projector_weights, preferred_element_type=jnp.float32
    ) / (EMBED_DIMENSION / 256.0 * softness_per_sequence[:, None])
    largest = lax.pmax(jnp.max(lexicon_logit_values, axis=1), ("dp", "mp"))
    total_exp = lax.psum(
        jnp.sum(jnp.exp(lexicon_logit_values - largest[:, None]), axis=1), ("dp", "mp")
    )
    logprobs = lexicon_logit_values - largest[:, None] - jnp.log(total_exp)[:, None]
    return (new_hidden, logprobs)


def solution(mesh):
    return jax.shard_map(
        body,
        mesh=mesh,
        in_specs=(
            P("dp", "mp"),
            P("dp", None),
            P("dp", None),
            P("mp"),
            P(),
            P(None, "dp", "mp"),
            P(None, "dp", "mp"),
            P(None, "mp", "dp"),
            P(),
            P(None, ("dp", "mp")),
            P(),
        ),
        out_specs=(P("dp", "mp"), P(None, ("dp", "mp"))),
        check_vma=False,
    )
```

profile of v0, /device:TPU:8, one launch (start us, length us, event | category | flops | bytes accessed | tf_op | source)
XLA Modules:
  0.0 1763.1 jit_solution(12189918322459456357)
XLA Ops:
  7.2 1.1 multiply_reduce_fusion
  8.4 44.8 %psum.21 = f32[256]{0:T(256)S(1)} all-reduce(f32[256]{0:T(256)S(1)} %multiply_reduce_fusion), channel_id=1, replica_groups=mesh['dp'=16,'mp'=16] {'mp'}, use_global_device_ids=true, to_apply=%region_5.6 | all-reduce | flops 256 | bytes 2048 | tf_op jit(solution)/shard_map/psum | solution.py:46
  53.2 1.6 multiply_convert_fusion
  54.9 1.8 fusion.124
  56.8 1.8 fusion.125
  58.7 0.8 fusion.126
  67.0 1.4 scatter_custom_fusion.5
  68.4 1.4 scatter_custom_fusion.4
  70.7 1.9 scatter_custom_fusion.6
  72.6 1.9 scatter_custom_fusion.2
  74.6 1.4 scatter_custom_fusion.1
  76.0 1.4 scatter_custom_fusion
  79.3 2.0 scatter_custom_fusion.10
  81.2 1.4 scatter_custom_fusion.9
  82.6 1.4 scatter_custom_fusion.8
  84.7 2.4 scatter_custom_fusion.14
  87.1 1.4 scatter_custom_fusion.13
  88.5 1.4 scatter_custom_fusion.12
  90.5 44.5 %all-gather.26.cloned.1.call-done = bf16[256,2304]{0,1:T(8,128)(2,1)} async-done(((bf16[256,144]{0,1:T(8,128)(2,1)}), bf16[256,2304]{0,1:T(8,128)(2,1)}) %all-gather.26.cloned.1.call-update) | async-done | bytes 1179664 | tf_op jit(solution)/shard_map/all_gather | solution.py:52
  135.1 1.5 fusion.128
  136.6 4.9 gather_fusion.9
  141.8 2.5 gather_fusion.3
  144.3 2.5 gather_fusion.1
  146.8 1.6 copy.22
  148.4 2.1 gather_fusion.2
  150.5 2.2 gather_fusion
  152.6 2.6 gather_fusion.5
  155.2 2.1 gather_fusion.4
  157.3 2.6 gather_fusion.7
  159.9 2.2 gather_fusion.6
  164.9 32.4 %all-gather.28.cloned.1.call-done = bf16[1,2304,360]{2,1,0:T(8,128)(2,1)} async-done(((bf16[1,144,360]{2,1,0:T(8,128)(2,1)}), bf16[1,2304,360]{2,1,0:T(8,128)(2,1)}) %all-gather.28.cloned.1.call-update) | async-done | bytes 1658896 | tf_op jit(solution)/shard_map/all_gather | solution.py:72
  197.3 2.3 fusion.18
  199.5 56.7 %all-gather.30.cloned.1.call-done = bf16[1,2304,360]{2,1,0:T(8,128)(2,1)} async-done(((bf16[1,144,360]{2,1,0:T(8,128)(2,1)}), bf16[1,2304,360]{2,1,0:T(8,128)(2,1)}) %all-gather.30.cloned.1.call-update) | async-done | bytes 1658896 | tf_op jit(solution)/shard_map/all_gather | solution.py:73
  256.3 58.8 %all-gather.32.cloned.1.call-done = bf16[1,360,2304]{1,2,0:T(8,128)(2,1)} async-done(((bf16[1,360,144]{1,2,0:T(8,128)(2,1)}), bf16[1,360,2304]{1,2,0:T(8,128)(2,1)}) %all-gather.32.cloned.1.call-update) | async-done | bytes 1658896 | tf_op jit(solution)/shard_map/all_gather | solution.py:84
  315.1 4.4 convolution_multiply_fusion.3
  319.5 5.2 scatter_custom_fusion.3
  324.7 49.2 %all-gather.34.cloned.1.call-done = bf16[1,2304,360]{2,1,0:T(8,128)(2,1)} async-done(((bf16[1,144,360]{2,1,0:T(8,128)(2,1)}), bf16[1,2304,360]{2,1,0:T(8,128)(2,1)}) %all-gather.34.cloned.1.call-update) | async-done | bytes 1658896 | tf_op jit(solution)/shard_map/all_gather | solution.py:72
  373.9 2.0 fusion.13
  375.9 56.8 %all-gather.36.cloned.1.call-done = bf16[1,2304,360]{2,1,0:T(8,128)(2,1)} async-done(((bf16[1,144,360]{2,1,0:T(8,128)(2,1)}), bf16[1,2304,360]{2,1,0:T(8,128)(2,1)}) %all-gather.36.cloned.1.call-update) | async-done | bytes 1658896 | tf_op jit(solution)/shard_map/all_gather | solution.py:73
  432.7 59.5 %all-gather.38.cloned.1.call-done = bf16[1,360,2304]{1,2,0:T(8,128)(2,1)} async-done(((bf16[1,360,144]{1,2,0:T(8,128)(2,1)}), bf16[1,360,2304]{1,2,0:T(8,128)(2,1)}) %all-gather.38.cloned.1.call-update) | async-done | bytes 1658896 | tf_op jit(solution)/shard_map/all_gather | solution.py:84
  492.3 4.4 convolution_multiply_fusion.2
  496.7 6.6 scatter_fusion
  503.2 48.0 %all-gather.40.cloned.1.call-done = bf16[1,2304,360]{2,1,0:T(8,128)(2,1)} async-done(((bf16[1,144,360]{2,1,0:T(8,128)(2,1)}), bf16[1,2304,360]{2,1,0:T(8,128)(2,1)}) %all-gather.40.cloned.1.call-update) | async-done | bytes 1658896 | tf_op jit(solution)/shard_map/all_gather | solution.py:72
  551.3 2.0 fusion.8
  553.3 57.0 %all-gather.42.cloned.1.call-done = bf16[1,2304,360]{2,1,0:T(8,128)(2,1)} async-done(((bf16[1,144,360]{2,1,0:T(8,128)(2,1)}), bf16[1,2304,360]{2,1,0:T(8,128)(2,1)}) %all-gather.42.cloned.1.call-update) | async-done | bytes 1658896 | tf_op jit(solution)/shard_map/all_gather | solution.py:73
  610.3 58.8 %all-gather.44.cloned.1.call-done = bf16[1,360,2304]{1,2,0:T(8,128)(2,1)} async-done(((bf16[1,360,144]{1,2,0:T(8,128)(2,1)}), bf16[1,360,2304]{1,2,0:T(8,128)(2,1)}) %all-gather.44.cloned.1.call-update) | async-done | bytes 1658896 | tf_op jit(solution)/shard_map/all_gather | solution.py:84
  669.1 4.4 convolution_multiply_fusion.1
  673.5 6.6 scatter_fusion.1
  680.0 48.0 %all-gather.46.cloned.1.call-done = bf16[1,2304,360]{2,1,0:T(8,128)(2,1)} async-done(((bf16[1,144,360]{2,1,0:T(8,128)(2,1)}), bf16[1,2304,360]{2,1,0:T(8,128)(2,1)}) %all-gather.46.cloned.1.call-update) | async-done | bytes 1658896 | tf_op jit(solution)/shard_map/all_gather | solution.py:72
  728.1 2.0 fusion.3
  730.1 56.8 %all-gather.48.cloned.1.call-done = bf16[1,2304,360]{2,1,0:T(8,128)(2,1)} async-done(((bf16[1,144,360]{2,1,0:T(8,128)(2,1)}), bf16[1,2304,360]{2,1,0:T(8,128)(2,1)}) %all-gather.48.cloned.1.call-update) | async-done | bytes 1658896 | tf_op jit(solution)/shard_map/all_gather | solution.py:73
  786.9 59.5 %all-gather.50.cloned.1.call-done = bf16[1,360,2304]{1,2,0:T(8,128)(2,1)} async-done(((bf16[1,360,144]{1,2,0:T(8,128)(2,1)}), bf16[1,360,2304]{1,2,0:T(8,128)(2,1)}) %all-gather.50.cloned.1.call-update) | async-done | bytes 1658896 | tf_op jit(solution)/shard_map/all_gather | solution.py:84
  846.5 4.4 convolution_multiply_fusion
  850.8 6.5 scatter_fusion.2
  857.3 1.8 convert_element_type.104
  859.1 1.4 copy.31
  860.5 1.0 copy.28
  861.8 0.8 dynamic_slice.3
  862.6 81.3 %reduce-scatter.4.cloned.1.call-done = bf16[144,256]{1,0:T(8,128)(2,1)} async-done(((bf16[2304,256]{1,0:T(8,128)(2,1)}), bf16[144,256]{1,0:T(8,128)(2,1)}) %reduce-scatter.4.cloned.1.call-update) | async-done | bytes 73744
  943.9 1.0 copy.32
  946.4 38.2 %psum.22 = f32[4]{0:T(128)S(1)} all-reduce(f32[4]{0:T(128)S(1)} %multiply_reduce_fusion.1), channel_id=1, replica_groups=mesh['dp'=16,'mp'=16] {'mp'}, use_global_device_ids=true, to_apply=%region_35.36 | all-reduce | flops 4 | bytes 32 | tf_op jit(solution)/shard_map/psum | solution.py:101
  984.7 546.4 %all_gather.55 = bf16[256,4,144]{2,1,0:T(4,128)(2,1)S(1)} all-gather(bf16[1,4,144]{2,1,0:T(4,128)(2,1)S(1)} %fusion.79), channel_id=1, replica_groups=mesh['dp'=16,'mp'=16] {'dp','mp'}, dimensions={0}, use_global_device_ids=true | all-gather | bytes 296064 | tf_op jit(solution)/shard_map/all_gather | solution.py:108
  1532.5 148.7 %pmax.7 = f32[64]{0:T(128)S(1)} all-reduce(f32[64]{0:T(128)S(1)} %get-tuple-element.38), channel_id=1, replica_groups=mesh['dp'=16,'mp'=16] {'dp','mp'}, use_global_device_ids=true, to_apply=%region_37.38 | all-reduce | flops 64 | bytes 512 | tf_op jit(solution)/shard_map/pmax | solution.py:117
  1681.3 74.2 %psum.23 = f32[64]{0:T(128)S(1)} all-reduce(f32[64]{0:T(128)S(1)} %exponential_reduce_fusion), channel_id=1, replica_groups=mesh['dp'=16,'mp'=16] {'dp','mp'}, use_global_device_ids=true, to_apply=%region_39.40 | all-reduce | flops 64 | bytes 512 | tf_op jit(solution)/shard_map/psum | solution.py:118
  (132 shorter events, 18.6 us)
Async XLA Ops:
  7.2 1524.7 %copy-start = (bf16[2304,512]{1,0:T(8,128)(2,1)S(1)}, bf16[2304,512]{1,0:T(8,128)(2,1)}, u32[]{:S(2)}) copy-start(bf16[2304,512]{1,0:T(8,128)(2,1)} %param.20) | copy-start | bytes 7077892
  7.2 51.5 %copy-start.5 = (bf16[4,360,144]{1,2,0:T(8,128)(2,1)S(1)}, bf16[4,360,144]{1,2,0:T(8,128)(2,1)}, u32[]{:S(2)}) copy-start(bf16[4,360,144]{1,2,0:T(8,128)(2,1)} %param.18) | copy-start | bytes 1244164
  7.2 127.9 %all-gather.26.cloned.1.call-start = ((), (), s32[]{:S(2)}) async-start(), calls=%async_computation.1 | async-start | bytes 1253376 | tf_op jit(solution)/shard_map/all_gather | solution.py:52
  54.8 142.4 %all-gather.28.cloned.1.call-start = ((), (), s32[]{:S(2)}) async-start(), calls=%async_computation.2 | async-start | bytes 1880064 | tf_op jit(solution)/shard_map/all_gather | solution.py:72
  56.7 8.9 copy-start.6
  56.7 78.3 %copy-start.7 = (bf16[2304,4]{0,1:T(4,128)(2,1)S(1)}, bf16[2304,4]{0,1:T(4,128)(2,1)}, u32[]{:S(2)}) copy-start(bf16[2304,4]{0,1:T(4,128)(2,1)} %param.15) | copy-start | bytes 55300
  56.7 199.5 %all-gather.30.cloned.1.call-start = ((), (), s32[]{:S(2)}) async-start(), calls=%async_computation.3 | async-start | bytes 1880064 | tf_op jit(solution)/shard_map/all_gather | solution.py:73
  58.7 256.4 %all-gather.32.cloned.1.call-start = ((), (), s32[]{:S(2)}) async-start(), calls=%async_computation.4 | async-start | bytes 1880064 | tf_op jit(solution)/shard_map/all_gather | solution.py:84
  59.5 314.4 %all-gather.34.cloned.1.call-start = ((), (), s32[]{:S(2)}) async-start(), calls=%async_computation.5 | async-start | bytes 1880064 | tf_op jit(solution)/shard_map/all_gather | solution.py:72
  60.1 372.6 %all-gather.36.cloned.1.call-start = ((), (), s32[]{:S(2)}) async-start(), calls=%async_computation.6 | async-start | bytes 1880064 | tf_op jit(solution)/shard_map/all_gather | solution.py:73
  60.7 431.6 %all-gather.38.cloned.1.call-start = ((), (), s32[]{:S(2)}) async-start(), calls=%async_computation.7 | async-start | bytes 1880064 | tf_op jit(solution)/shard_map/all_gather | solution.py:84
  61.4 489.8 %all-gather.40.cloned.1.call-start = ((), (), s32[]{:S(2)}) async-start(), calls=%async_computation.8 | async-start | bytes 1880064 | tf_op jit(solution)/shard_map/all_gather | solution.py:72
  62.2 548.1 %all-gather.42.cloned.1.call-start = ((), (), s32[]{:S(2)}) async-start(), calls=%async_computation.9 | async-start | bytes 1880064 | tf_op jit(solution)/shard_map/all_gather | solution.py:73
  62.9 606.2 %all-gather.44.cloned.1.call-start = ((), (), s32[]{:S(2)}) async-start(), calls=%async_computation.10 | async-start | bytes 1880064 | tf_op jit(solution)/shard_map/all_gather | solution.py:84
  63.5 664.5 %all-gather.46.cloned.1.call-start = ((), (), s32[]{:S(2)}) async-start(), calls=%async_computation.11 | async-start | bytes 1880064 | tf_op jit(solution)/shard_map/all_gather | solution.py:72
  64.3 722.6 %all-gather.48.cloned.1.call-start = ((), (), s32[]{:S(2)}) async-start(), calls=%async_computation.12 | async-start | bytes 1880064 | tf_op jit(solution)/shard_map/all_gather | solution.py:73
  64.8 781.6 %all-gather.50.cloned.1.call-start = ((), (), s32[]{:S(2)}) async-start(), calls=%async_computation.13 | async-start | bytes 1880064 | tf_op jit(solution)/shard_map/all_gather | solution.py:84
  65.6 878.4 %reduce-scatter.4.cloned.1.call-start = ((), (), s32[]{:S(2)}) async-start(), calls=%async_computation.14 | async-start | bytes 1253376
  77.4 0.6 copy-start.14
  84.1 4.4 copy-start.10
  89.9 45.2 %copy-start.8 = (s32[160]{0:T(256)}, s32[160]{0:T(256)S(1)}, u32[]{:S(2)}) copy-start(s32[160]{0:T(256)S(1)} %get-tuple-element.31) | copy-start | bytes 1924
  159.9 2.2 copy-start.12
  159.9 3.0 copy-start.13
  162.1 153.0 %copy-start.4 = (bf16[160,2304]{1,0:T(8,128)(2,1)S(1)}, bf16[160,2304]{1,0:T(8,128)(2,1)}, u32[]{:S(2)}) copy-start(bf16[160,2304]{1,0:T(8,128)(2,1)} %gather_fusion) | copy-start | bytes 2211844
  319.5 54.4 %copy-start.3 = (bf16[160,2304]{1,0:T(8,128)(2,1)S(1)}, bf16[160,2304]{1,0:T(8,128)(2,1)}, u32[]{:S(2)}) copy-start(bf16[160,2304]{1,0:T(8,128)(2,1)} %gather_fusion.2) | copy-start | bytes 2211844
  496.7 54.6 %copy-start.2 = (bf16[160,2304]{1,0:T(8,128)(2,1)S(1)}, bf16[160,2304]{1,0:T(8,128)(2,1)}, u32[]{:S(2)}) copy-start(bf16[160,2304]{1,0:T(8,128)(2,1)} %gather_fusion.4) | copy-start | bytes 2211844
  553.3 120.2 %copy-start.11 = (s32[160]{0:T(256)S(1)}, s32[160]{0:T(256)}, u32[]{:S(2)}) copy-start(s32[160]{0:T(256)} %copy-done.10) | copy-start | bytes 1924
  673.5 54.6 %copy-start.1 = (bf16[160,2304]{1,0:T(8,128)(2,1)S(1)}, bf16[160,2304]{1,0:T(8,128)(2,1)}, u32[]{:S(2)}) copy-start(bf16[160,2304]{1,0:T(8,128)(2,1)} %gather_fusion.6) | copy-start | bytes 2211844
  730.1 120.7 %copy-start.9 = (s32[160]{0:T(256)S(1)}, s32[160]{0:T(256)}, u32[]{:S(2)}) copy-start(s32[160]{0:T(256)} %copy-done.8) | copy-start | bytes 1924
  859.1 2.5 copy-start.15
  859.1 3.5 copy-start.16
Sparse Core Ops, SparseCore 0:
  54.9 80.0 all-gather.25
  137.7 59.5 all-gather.27
  199.9 56.3 all-gather.29
  258.7 56.3 all-gather.31
  317.5 56.3 all-gather.33
  376.4 56.3 all-gather.35
  435.9 56.3 all-gather.37
  494.9 56.3 all-gather.39
  553.9 56.3 all-gather.41
  612.7 56.3 all-gather.43
  671.7 56.3 all-gather.45
  730.5 56.3 all-gather.47
  790.1 56.3 all-gather.49
  860.7 83.2 reduce-scatter.3
where the time goes:
time: 1770 us; the launch traced here: 1760 us
  blocking collectives  852 us (48%)
  waiting for transfers between devices  773 us (44%)
  local copies, waits for them, and re-layouts  56.7 us (3%)
  other arithmetic  37.7 us (2%)
  matrix products  28 us (2%)
    all_gather x1, blocking collectives, body(): lax.all_gather(end_normed[None], ('dp', 'mp'), axis=0, tiled=True)  546 us
    all_gather x4, waiting for transfers between devices, body(): lax.all_gather(specialist_contract_weights[expert], 'dp', axis=1, tiled=T...  237 us
    all_gather x4, waiting for transfers between devices, body(): lax.all_gather(specialist_expand_weights[expert], 'dp', axis=0, tiled=True)  227 us
    all_gather x4, waiting for transfers between devices, body(): lax.all_gather(specialist_switch_weights[expert], 'dp', axis=0, tiled=True)  178 us
    pmax x1, blocking collectives, body(): largest = lax.pmax(jnp.max(lexicon_logit_values, axis=1), ('dp', 'mp'))  149 us
    unnamed x15, waiting for transfers between devices  87 us
    psum x1, blocking collectives, body(): lax.psum(jnp.sum(jnp.exp(lexicon_logit_values - largest[:, None]), axis=1...  74.2 us
    psum x1, blocking collectives, body(): lax.psum(jnp.sum(skip_stream_arriving * skip_stream_arriving, axis=1), 'mp')  44.8 us
  transfers between devices with their start and end apart: 14, of which 14 were waited for; matrix products, arithmetic and copies ran while one was open for 6% of the time, Pallas kernels for 0%

commit v1 on v0

--- a/solution.py
+++ b/solution.py
@@ -95,29 +95,23 @@
     new_hidden = skip_stream_arriving + branch_scale * branch
     ends_index = jnp.cumsum(sequence_piece_tallies[0], dtype=jnp.int32) - 1
     end_local = new_hidden[ends_index]
-    groups = lax.axis_size("dp")
-    columns_count = lax.axis_size("mp")
-    req_count = ends_index.shape[0]
-    end_squares = lax.psum(jnp.sum(end_local * end_local, axis=1), "mp")
-    gain_local = lax.dynamic_slice_in_dim(
-        terminal_rmsnorm_gain, lax.axis_index("mp") * local_width, local_width
-    )
+    end_rows = lax.all_gather(end_local, "mp", axis=1, tiled=True)
+    end_squares = jnp.sum(end_rows * end_rows, axis=1)
     end_normed = (
-        end_local * lax.rsqrt(end_squares / EMBED_DIMENSION + epsilon)[:, None] * gain_local
+        end_rows * lax.rsqrt(end_squares / EMBED_DIMENSION + epsilon)[:, None] * terminal_rmsnorm_gain
     ).astype(jnp.bfloat16)
-    shaped = lax.all_gather(end_normed[None], ("dp", "mp"), axis=0, tiled=True).reshape(
-        groups, columns_count, req_count, local_width
-    )
-    lexicon_projector_feed = shaped.transpose(0, 2, 1, 3).reshape(
-        groups * req_count, columns_count * local_width
-    )
+    lexicon_projector_feed = lax.all_gather(end_normed, "dp", axis=0, tiled=True)
     lexicon_logit_values = jnp.dot(
         lexicon_projector_feed, lexicon_projector_weights, preferred_element_type=jnp.float32
     ) / (EMBED_DIMENSION / 256.0 * softness_per_sequence[:, None])
-    largest = lax.pmax(jnp.max(lexicon_logit_values, axis=1), ("dp", "mp"))
-    total_exp = lax.psum(
-        jnp.sum(jnp.exp(lexicon_logit_values - largest[:, None]), axis=1), ("dp", "mp")
-    )
+    local_max = jnp.max(lexicon_logit_values, axis=1)
+    local_sum = jnp.sum(jnp.exp(lexicon_logit_values - local_max[:, None]), axis=1)
+    stats = jnp.stack([local_max, local_sum])
+    for axis in ("mp", "dp"):
+        held = lax.all_gather(stats, axis, axis=0)
+        top = jnp.max(held[:, 0], axis=0)
+        stats = jnp.stack([top, jnp.sum(held[:, 1] * jnp.exp(held[:, 0] - top[None]), axis=0)])
+    largest, total_exp = stats[0], stats[1]
     logprobs = lexicon_logit_values - largest[:, None] - jnp.log(total_exp)[:, None]
     return (new_hidden, logprobs)
 

time: 1770 us -> 1090 us (0.62)
  blocking collectives: 852 us -> 174 us
    all_gather x1 -> x4, blocking collectives: 546 us -> 129 us  [the longest x2 60.8 us: body(): held = lax.all_gather(stats, axis, axis=0)]
    pmax x1 -> x0, blocking collectives: 149 us -> none  [body(): largest = lax.pmax(jnp.max(lexicon_logit_values, axis=1), ('dp', 'mp'))]
    psum x2 -> x0, blocking collectives: 112 us -> none  [the longest x1 74.2 us: body(): lax.psum(jnp.sum(jnp.exp(lexicon_logit_values - largest[:, None]), axis=1...]
  transfers between devices with their start and end apart: 14 -> 14, of which waited for: 14 -> 14; matrix products, arithmetic and copies ran while one was open for 6% -> 9% of each run, Pallas kernels for 0% -> 0%
where the time goes in v1:
time: 1090 us; the launch traced here: 1080 us
  waiting for transfers between devices  775 us (71%)
  blocking collectives  174 us (16%)
  local copies, waits for them, and re-layouts  55 us (5%)
  other arithmetic  37.7 us (3%)
  matrix products  28 us (3%)
  between operations  14.4 us (1%)
    all_gather x4, waiting for transfers between devices, body(): lax.all_gather(specialist_contract_weights[expert], 'dp', axis=1, tiled=T...  237 us
    all_gather x4, waiting for transfers between devices, body(): lax.all_gather(specialist_expand_weights[expert], 'dp', axis=0, tiled=True)  227 us
    all_gather x4, waiting for transfers between devices, body(): lax.all_gather(specialist_switch_weights[expert], 'dp', axis=0, tiled=True)  178 us
    unnamed x15, waiting for transfers between devices  87.8 us
    all_gather x2, blocking collectives, body(): held = lax.all_gather(stats, axis, axis=0)  60.8 us
    all_gather x1, waiting for transfers between devices, body(): features = lax.all_gather(normed_local, 'mp', axis=1, tiled=True)  45 us
    psum x1, blocking collectives, body(): lax.psum(jnp.sum(skip_stream_arriving * skip_stream_arriving, axis=1), 'mp')  44.8 us
    all_gather x1, blocking collectives, body(): end_rows = lax.all_gather(end_local, 'mp', axis=1, tiled=True)  37.5 us
  transfers between devices with their start and end apart: 14, of which 14 were waited for; matrix products, arithmetic and copies ran while one was open for 9% of the time, Pallas kernels for 0%

profile of v1, /device:TPU:8, one launch (start us, length us, event | category | flops | bytes accessed | tf_op | source)
XLA Modules:
  0.0 1083.7 jit_solution(11176963548852286973)
XLA Ops:
  7.2 1.1 multiply_reduce_fusion
  8.4 44.8 %psum.7 = f32[256]{0:T(256)S(1)} all-reduce(f32[256]{0:T(256)S(1)} %multiply_reduce_fusion), channel_id=1, replica_groups=mesh['dp'=16,'mp'=16] {'mp'}, use_global_device_ids=true, to_apply=%region_5.6 | all-reduce | flops 256 | bytes 2048 | tf_op jit(solution)/shard_map/psum | solution.py:46
  53.2 1.6 multiply_convert_fusion
  54.9 1.8 fusion.123
  56.8 1.8 fusion.124
  58.7 0.8 fusion.125
  67.0 1.4 scatter_custom_fusion.5
  68.4 1.4 scatter_custom_fusion.4
  70.7 1.9 scatter_custom_fusion.6
  72.6 1.9 scatter_custom_fusion.2
  74.6 1.4 scatter_custom_fusion.1
  76.0 1.4 scatter_custom_fusion
  79.3 2.0 scatter_custom_fusion.10
  81.2 1.4 scatter_custom_fusion.9
  82.6 1.4 scatter_custom_fusion.8
  84.7 1.9 scatter_custom_fusion.14
  86.6 1.4 scatter_custom_fusion.13
  88.0 1.4 scatter_custom_fusion.12
  90.1 45.0 %all-gather.33.cloned.1.call-done = bf16[256,2304]{0,1:T(8,128)(2,1)} async-done(((bf16[256,144]{0,1:T(8,128)(2,1)}), bf16[256,2304]{0,1:T(8,128)(2,1)}) %all-gather.33.cloned.1.call-update) | async-done | bytes 1179664 | tf_op jit(solution)/shard_map/all_gather | solution.py:52
  135.0 1.5 fusion.127
  136.6 4.9 gather_fusion.9
  141.7 2.5 gather_fusion.3
  144.3 2.5 gather_fusion.1
  146.8 1.6 copy.26
  148.4 2.1 gather_fusion.2
  150.5 2.2 gather_fusion
  152.6 2.6 gather_fusion.5
  155.2 2.1 gather_fusion.4
  157.3 2.6 gather_fusion.7
  159.9 2.2 gather_fusion.6
  164.9 32.2 %all-gather.35.cloned.1.call-done = bf16[1,2304,360]{2,1,0:T(8,128)(2,1)} async-done(((bf16[1,144,360]{2,1,0:T(8,128)(2,1)}), bf16[1,2304,360]{2,1,0:T(8,128)(2,1)}) %all-gather.35.cloned.1.call-update) | async-done | bytes 1658896 | tf_op jit(solution)/shard_map/all_gather | solution.py:72
  197.1 2.3 fusion.18
  199.3 56.7 %all-gather.37.cloned.1.call-done = bf16[1,2304,360]{2,1,0:T(8,128)(2,1)} async-done(((bf16[1,144,360]{2,1,0:T(8,128)(2,1)}), bf16[1,2304,360]{2,1,0:T(8,128)(2,1)}) %all-gather.37.cloned.1.call-update) | async-done | bytes 1658896 | tf_op jit(solution)/shard_map/all_gather | solution.py:73
  256.1 58.8 %all-gather.39.cloned.1.call-done = bf16[1,360,2304]{1,2,0:T(8,128)(2,1)} async-done(((bf16[1,360,144]{1,2,0:T(8,128)(2,1)}), bf16[1,360,2304]{1,2,0:T(8,128)(2,1)}) %all-gather.39.cloned.1.call-update) | async-done | bytes 1658896 | tf_op jit(solution)/shard_map/all_gather | solution.py:84
  314.9 4.4 convolution_multiply_fusion.3
  319.3 5.0 scatter_custom_fusion.3
  324.4 49.4 %all-gather.41.cloned.1.call-done = bf16[1,2304,360]{2,1,0:T(8,128)(2,1)} async-done(((bf16[1,144,360]{2,1,0:T(8,128)(2,1)}), bf16[1,2304,360]{2,1,0:T(8,128)(2,1)}) %all-gather.41.cloned.1.call-update) | async-done | bytes 1658896 | tf_op jit(solution)/shard_map/all_gather | solution.py:72
  373.7 2.0 fusion.13
  375.8 56.8 %all-gather.43.cloned.1.call-done = bf16[1,2304,360]{2,1,0:T(8,128)(2,1)} async-done(((bf16[1,144,360]{2,1,0:T(8,128)(2,1)}), bf16[1,2304,360]{2,1,0:T(8,128)(2,1)}) %all-gather.43.cloned.1.call-update) | async-done | bytes 1658896 | tf_op jit(solution)/shard_map/all_gather | solution.py:73
  432.6 59.5 %all-gather.45.cloned.1.call-done = bf16[1,360,2304]{1,2,0:T(8,128)(2,1)} async-done(((bf16[1,360,144]{1,2,0:T(8,128)(2,1)}), bf16[1,360,2304]{1,2,0:T(8,128)(2,1)}) %all-gather.45.cloned.1.call-update) | async-done | bytes 1658896 | tf_op jit(solution)/shard_map/all_gather | solution.py:84
  492.1 4.4 convolution_multiply_fusion.2
  496.5 6.6 scatter_fusion
  503.1 48.0 %all-gather.47.cloned.1.call-done = bf16[1,2304,360]{2,1,0:T(8,128)(2,1)} async-done(((bf16[1,144,360]{2,1,0:T(8,128)(2,1)}), bf16[1,2304,360]{2,1,0:T(8,128)(2,1)}) %all-gather.47.cloned.1.call-update) | async-done | bytes 1658896 | tf_op jit(solution)/shard_map/all_gather | solution.py:72
  551.1 2.0 fusion.8
  553.1 57.0 %all-gather.49.cloned.1.call-done = bf16[1,2304,360]{2,1,0:T(8,128)(2,1)} async-done(((bf16[1,144,360]{2,1,0:T(8,128)(2,1)}), bf16[1,2304,360]{2,1,0:T(8,128)(2,1)}) %all-gather.49.cloned.1.call-update) | async-done | bytes 1658896 | tf_op jit(solution)/shard_map/all_gather | solution.py:73
  610.1 58.8 %all-gather.51.cloned.1.call-done = bf16[1,360,2304]{1,2,0:T(8,128)(2,1)} async-done(((bf16[1,360,144]{1,2,0:T(8,128)(2,1)}), bf16[1,360,2304]{1,2,0:T(8,128)(2,1)}) %all-gather.51.cloned.1.call-update) | async-done | bytes 1658896 | tf_op jit(solution)/shard_map/all_gather | solution.py:84
  668.9 4.4 convolution_multiply_fusion.1
  673.3 6.6 scatter_fusion.1
  679.9 48.0 %all-gather.53.cloned.1.call-done = bf16[1,2304,360]{2,1,0:T(8,128)(2,1)} async-done(((bf16[1,144,360]{2,1,0:T(8,128)(2,1)}), bf16[1,2304,360]{2,1,0:T(8,128)(2,1)}) %all-gather.53.cloned.1.call-update) | async-done | bytes 1658896 | tf_op jit(solution)/shard_map/all_gather | solution.py:72
  727.9 2.0 fusion.3
  729.9 56.8 %all-gather.55.cloned.1.call-done = bf16[1,2304,360]{2,1,0:T(8,128)(2,1)} async-done(((bf16[1,144,360]{2,1,0:T(8,128)(2,1)}), bf16[1,2304,360]{2,1,0:T(8,128)(2,1)}) %all-gather.55.cloned.1.call-update) | async-done | bytes 1658896 | tf_op jit(solution)/shard_map/all_gather | solution.py:73
  786.7 59.5 %all-gather.57.cloned.1.call-done = bf16[1,360,2304]{1,2,0:T(8,128)(2,1)} async-done(((bf16[1,360,144]{1,2,0:T(8,128)(2,1)}), bf16[1,360,2304]{1,2,0:T(8,128)(2,1)}) %all-gather.57.cloned.1.call-update) | async-done | bytes 1658896 | tf_op jit(solution)/shard_map/all_gather | solution.py:84
  846.3 4.3 convolution_multiply_fusion
  850.6 6.5 scatter_fusion.2
  857.1 1.8 convert_element_type.97
  858.9 1.4 copy.37
  860.4 1.0 copy.32
  861.6 82.2 %reduce-scatter.4.cloned.1.call-done = bf16[144,256]{1,0:T(8,128)(2,1)} async-done(((bf16[2304,256]{1,0:T(8,128)(2,1)}), bf16[144,256]{1,0:T(8,128)(2,1)}) %reduce-scatter.4.cloned.1.call-update) | async-done | bytes 73744
  943.8 1.0 copy.38
  944.9 0.8 copy.36
  946.2 37.5 %all-gather.15 = f32[16,144,4]{1,2,0:T(4,128)S(1)} all-gather(f32[1,144,4]{1,2,0:T(4,128)S(1)} %bitcast.132), channel_id=14, replica_groups=mesh['dp'=16,'mp'=16] {'mp'}, dimensions={0}, use_global_device_ids=true | all-gather | bytes 39168 | tf_op jit(solution)/shard_map/all_gather | solution.py:98
  984.1 30.4 %all-gather.16 = bf16[16,4,2304]{2,1,0:T(4,128)(2,1)S(1)} all-gather(bf16[1,4,2304]{2,1,0:T(4,128)(2,1)S(1)} %fusion.78), channel_id=1, replica_groups=mesh['dp'=16,'mp'=16] {'dp'}, dimensions={0}, use_global_device_ids=true | all-gather | bytes 313344 | tf_op jit(solution)/shard_map/all_gather | solution.py:103
  1015.5 36.8 %all-gather.17 = f32[16,2,64]{2,1,0:T(2,128)S(1)} all-gather(f32[1,2,64]{2,1,0:T(2,128)S(1)} %maximum_bitcast_fusion), channel_id=15, replica_groups=mesh['dp'=16,'mp'=16] {'mp'}, dimensions={0}, use_global_device_ids=true | all-gather | bytes 8704 | tf_op jit(solution)/shard_map/all_gather | solution.py:111
  1052.3 24.0 %all-gather.18 = f32[16,2,64]{2,1,0:T(2,128)S(1)} all-gather(f32[1,2,64]{2,1,0:T(2,128)S(1)} %maximum_bitcast_fusion.1), channel_id=16, replica_groups=mesh['dp'=16,'mp'=16] {'dp'}, dimensions={0}, use_global_device_ids=true | all-gather | bytes 8704 | tf_op jit(solution)/shard_map/all_gather | solution.py:111
  (140 shorter events, 17.5 us)
Async XLA Ops:
  7.2 1007.5 %copy-start = (bf16[2304,512]{1,0:T(8,128)(2,1)S(1)}, bf16[2304,512]{1,0:T(8,128)(2,1)}, u32[]{:S(2)}) copy-start(bf16[2304,512]{1,0:T(8,128)(2,1)} %param.20) | copy-start | bytes 7077892
  7.2 51.5 %copy-start.5 = (bf16[4,360,144]{1,2,0:T(8,128)(2,1)S(1)}, bf16[4,360,144]{1,2,0:T(8,128)(2,1)}, u32[]{:S(2)}) copy-start(bf16[4,360,144]{1,2,0:T(8,128)(2,1)} %param.18) | copy-start | bytes 1244164
  7.2 127.9 %all-gather.33.cloned.1.call-start = ((), (), s32[]{:S(2)}) async-start(), calls=%async_computation.1 | async-start | bytes 1253376 | tf_op jit(solution)/shard_map/all_gather | solution.py:52
  54.8 142.3 %all-gather.35.cloned.1.call-start = ((), (), s32[]{:S(2)}) async-start(), calls=%async_computation.2 | async-start | bytes 1880064 | tf_op jit(solution)/shard_map/all_gather | solution.py:72
  56.7 8.9 copy-start.6
  56.7 78.3 %copy-start.7 = (bf16[2304,4]{0,1:T(4,128)(2,1)S(1)}, bf16[2304,4]{0,1:T(4,128)(2,1)}, u32[]{:S(2)}) copy-start(bf16[2304,4]{0,1:T(4,128)(2,1)} %param.15) | copy-start | bytes 55300
  56.7 199.3 %all-gather.37.cloned.1.call-start = ((), (), s32[]{:S(2)}) async-start(), calls=%async_computation.3 | async-start | bytes 1880064 | tf_op jit(solution)/shard_map/all_gather | solution.py:73
  58.7 256.2 %all-gather.39.cloned.1.call-start = ((), (), s32[]{:S(2)}) async-start(), calls=%async_computation.4 | async-start | bytes 1880064 | tf_op jit(solution)/shard_map/all_gather | solution.py:84
  59.5 314.2 %all-gather.41.cloned.1.call-start = ((), (), s32[]{:S(2)}) async-start(), calls=%async_computation.5 | async-start | bytes 1880064 | tf_op jit(solution)/shard_map/all_gather | solution.py:72
  60.1 372.4 %all-gather.43.cloned.1.call-start = ((), (), s32[]{:S(2)}) async-start(), calls=%async_computation.6 | async-start | bytes 1880064 | tf_op jit(solution)/shard_map/all_gather | solution.py:73
  60.7 431.4 %all-gather.45.cloned.1.call-start = ((), (), s32[]{:S(2)}) async-start(), calls=%async_computation.7 | async-start | bytes 1880064 | tf_op jit(solution)/shard_map/all_gather | solution.py:84
  61.4 489.6 %all-gather.47.cloned.1.call-start = ((), (), s32[]{:S(2)}) async-start(), calls=%async_computation.8 | async-start | bytes 1880064 | tf_op jit(solution)/shard_map/all_gather | solution.py:72
  62.2 547.9 %all-gather.49.cloned.1.call-start = ((), (), s32[]{:S(2)}) async-start(), calls=%async_computation.9 | async-start | bytes 1880064 | tf_op jit(solution)/shard_map/all_gather | solution.py:73
  62.9 606.0 %all-gather.51.cloned.1.call-start = ((), (), s32[]{:S(2)}) async-start(), calls=%async_computation.10 | async-start | bytes 1880064 | tf_op jit(solution)/shard_map/all_gather | solution.py:84
  63.5 664.4 %all-gather.53.cloned.1.call-start = ((), (), s32[]{:S(2)}) async-start(), calls=%async_computation.11 | async-start | bytes 1880064 | tf_op jit(solution)/shard_map/all_gather | solution.py:72
  64.3 722.5 %all-gather.55.cloned.1.call-start = ((), (), s32[]{:S(2)}) async-start(), calls=%async_computation.12 | async-start | bytes 1880064 | tf_op jit(solution)/shard_map/all_gather | solution.py:73
  64.8 781.4 %all-gather.57.cloned.1.call-start = ((), (), s32[]{:S(2)}) async-start(), calls=%async_computation.13 | async-start | bytes 1880064 | tf_op jit(solution)/shard_map/all_gather | solution.py:84
  65.6 878.3 %reduce-scatter.4.cloned.1.call-start = ((), (), s32[]{:S(2)}) async-start(), calls=%async_computation.14 | async-start | bytes 1253376
  77.4 0.6 copy-start.15
  84.1 4.0 copy-start.11
  89.5 45.6 %copy-start.9 = (s32[160]{0:T(256)}, s32[160]{0:T(256)S(1)}, u32[]{:S(2)}) copy-start(s32[160]{0:T(256)S(1)} %get-tuple-element.37) | copy-start | bytes 1924
  159.9 2.2 copy-start.13
  159.9 3.0 copy-start.14
  162.1 152.8 %copy-start.4 = (bf16[160,2304]{1,0:T(8,128)(2,1)S(1)}, bf16[160,2304]{1,0:T(8,128)(2,1)}, u32[]{:S(2)}) copy-start(bf16[160,2304]{1,0:T(8,128)(2,1)} %gather_fusion) | copy-start | bytes 2211844
  319.3 54.4 %copy-start.3 = (bf16[160,2304]{1,0:T(8,128)(2,1)S(1)}, bf16[160,2304]{1,0:T(8,128)(2,1)}, u32[]{:S(2)}) copy-start(bf16[160,2304]{1,0:T(8,128)(2,1)} %gather_fusion.2) | copy-start | bytes 2211844
  496.5 54.6 %copy-start.2 = (bf16[160,2304]{1,0:T(8,128)(2,1)S(1)}, bf16[160,2304]{1,0:T(8,128)(2,1)}, u32[]{:S(2)}) copy-start(bf16[160,2304]{1,0:T(8,128)(2,1)} %gather_fusion.4) | copy-start | bytes 2211844
  553.1 120.2 %copy-start.12 = (s32[160]{0:T(256)S(1)}, s32[160]{0:T(256)}, u32[]{:S(2)}) copy-start(s32[160]{0:T(256)} %copy-done.11) | copy-start | bytes 1924
  673.3 54.6 %copy-start.1 = (bf16[160,2304]{1,0:T(8,128)(2,1)S(1)}, bf16[160,2304]{1,0:T(8,128)(2,1)}, u32[]{:S(2)}) copy-start(bf16[160,2304]{1,0:T(8,128)(2,1)} %gather_fusion.6) | copy-start | bytes 2211844
  729.9 120.7 %copy-start.10 = (s32[160]{0:T(256)S(1)}, s32[160]{0:T(256)}, u32[]{:S(2)}) copy-start(s32[160]{0:T(256)} %copy-done.9) | copy-start | bytes 1924
  858.9 2.5 copy-start.16
  858.9 2.7 copy-start.17
  860.3 123.7 %copy-start.8 = (f32[2304]{0:T(1024)S(1)}, f32[2304]{0:T(1024)}, u32[]{:S(2)}) copy-start(f32[2304]{0:T(1024)} %param.19) | copy-start | bytes 27652
Sparse Core Ops, SparseCore 0:
  54.9 80.0 all-gather.32
  137.7 59.3 all-gather.34
  199.7 56.3 all-gather.36
  258.5 56.3 all-gather.38
  317.4 56.3 all-gather.40
  376.2 56.3 all-gather.42
  435.8 56.3 all-gather.44
  494.7 56.3 all-gather.46
  553.7 56.3 all-gather.48
  612.5 56.3 all-gather.50
  671.5 56.3 all-gather.52
  730.4 56.3 all-gather.54
  789.9 56.3 all-gather.56
  860.5 83.3 reduce-scatter.3

commit v2 on v1

--- a/solution.py
+++ b/solution.py
@@ -55,36 +55,18 @@
     tables = [slot_tables(chosen_specialists, expert, CAP) for expert in range(experts)]
     inputs = jnp.stack([features[table[0]] for table in tables])
     scales = jnp.stack([mixing[table[0], table[2]] * table[1] for table in tables])
+    pair_weights = lax.all_gather(
+        jnp.stack([specialist_switch_weights, specialist_expand_weights], axis=1),
+        "dp", axis=2, tiled=True,
+    )
+    down_weights = lax.all_gather(specialist_contract_weights, "dp", axis=2, tiled=True)
     pieces_out = []
     for expert in range(experts):
         rows_in = inputs[expert]
-
-        def add_pair(carry, pieces, start, rows_in=rows_in):
-            return (
-                jnp.dot(rows_in, pieces[0], preferred_element_type=jnp.float32),
-                jnp.dot(rows_in, pieces[1], preferred_element_type=jnp.float32),
-            )
-
-        empty = jnp.zeros((CAP, unit_cols), jnp.float32)
-        gate, up_part = add_pair(
-            (empty, empty),
-            (
-                lax.all_gather(specialist_switch_weights[expert], "dp", axis=0, tiled=True),
-                lax.all_gather(specialist_expand_weights[expert], "dp", axis=0, tiled=True),
-            ),
-            jnp.int32(0),
-        )
+        gate = jnp.dot(rows_in, pair_weights[expert, 0], preferred_element_type=jnp.float32)
+        up_part = jnp.dot(rows_in, pair_weights[expert, 1], preferred_element_type=jnp.float32)
         act = (jax.nn.silu(gate) * up_part).astype(jnp.bfloat16)
-
-        def project(piece, start, act=act):
-            return jnp.dot(act, piece, preferred_element_type=jnp.float32)
-
-        pieces_out.append(
-            project(
-                lax.all_gather(specialist_contract_weights[expert], "dp", axis=1, tiled=True),
-                jnp.int32(0),
-            )
-        )
+        pieces_out.append(jnp.dot(act, down_weights[expert], preferred_element_type=jnp.float32))
     outputs = jnp.stack(pieces_out)
     combined = jnp.zeros((tok_rows, EMBED_DIMENSION), jnp.float32)
     for expert in range(experts):

time: 1090 us -> 664 us (0.61)
  waiting for transfers between devices: 775 us -> 354 us
    all_gather x12 -> x2, waiting for transfers between devices: 642 us -> 218 us  [the longest x1 124 us: body(): lax.all_gather(jnp.stack([specialist_switch_weights, specialist_expand_we...]
    unnamed x15 -> x5, waiting for transfers between devices: 87.8 us -> 82.6 us
  transfers between devices with their start and end apart: 14 -> 4, of which waited for: 14 -> 4; matrix products, arithmetic and copies ran while one was open for 9% -> 9% of each run, Pallas kernels for 0% -> 0%
where the time goes in v2:
time: 664 us; the launch traced here: 660 us
  waiting for transfers between devices  354 us (53%)
  blocking collectives  174 us (26%)
  local copies, waits for them, and re-layouts  50.6 us (8%)
  other arithmetic  39.5 us (6%)
  matrix products  27.9 us (4%)
  between operations  14.1 us (2%)
    all_gather x1, waiting for transfers between devices, body(): lax.all_gather(jnp.stack([specialist_switch_weights, specialist_expand_we...  124 us
    all_gather x1, waiting for transfers between devices, body(): lax.all_gather(specialist_contract_weights, 'dp', axis=2, tiled=True)  93.7 us
    unnamed x5, waiting for transfers between devices  82.6 us
    all_gather x2, blocking collectives, body(): held = lax.all_gather(stats, axis, axis=0)  60.8 us
    all_gather x1, waiting for transfers between devices, body(): features = lax.all_gather(normed_local, 'mp', axis=1, tiled=True)  53.4 us
    psum x1, blocking collectives, body(): lax.psum(jnp.sum(skip_stream_arriving * skip_stream_arriving, axis=1), 'mp')  44.8 us
    all_gather x1, blocking collectives, body(): end_rows = lax.all_gather(end_local, 'mp', axis=1, tiled=True)  37.8 us
    all_gather x1, blocking collectives, body(): lax.all_gather(end_normed, 'dp', axis=0, tiled=True)  30.4 us
  transfers between devices with their start and end apart: 4, of which 4 were waited for; matrix products, arithmetic and copies ran while one was open for 9% of the time, Pallas kernels for 0%

profile of v2, /device:TPU:8, one launch (start us, length us, event | category | flops | bytes accessed | tf_op | source)
XLA Modules:
  0.0 660.0 jit_solution(15968356792673381213)
XLA Ops:
  7.2 1.1 multiply_reduce_fusion
  8.3 44.8 %psum.7 = f32[256]{0:T(256)S(1)} all-reduce(f32[256]{0:T(256)S(1)} %multiply_reduce_fusion), channel_id=1, replica_groups=mesh['dp'=16,'mp'=16] {'mp'}, use_global_device_ids=true, to_apply=%region_5.6 | all-reduce | flops 256 | bytes 2048 | tf_op jit(solution)/shard_map/psum | solution.py:46
  53.1 1.6 multiply_convert_fusion
  54.9 2.2 pad_maximum_fusion
  57.2 0.7 all-gather.15.cloned.1.call-update
  58.4 0.3 reduce-window.40
  59.6 1.4 scatter_custom_fusion
  61.0 2.0 scatter_custom_fusion.2
  63.0 1.9 scatter_custom_fusion.6
  64.9 1.4 scatter_custom_fusion.4
  67.2 1.9 scatter_custom_fusion.10
  69.1 1.4 scatter_custom_fusion.8
  70.5 1.9 scatter_custom_fusion.14
  72.4 1.4 scatter_custom_fusion.12
  73.9 1.4 scatter_custom_fusion.9
  75.3 1.4 scatter_custom_fusion.5
  76.7 1.6 scatter_custom_fusion.13
  78.2 1.4 scatter_custom_fusion.1
  80.0 0.6 pad_clamp_fusion.3
  80.6 0.6 pad_clamp_fusion.1
  81.2 0.6 pad_clamp_fusion.4
  81.8 53.4 %all-gather.11.cloned.1.call-done = bf16[256,2304]{0,1:T(8,128)(2,1)} async-done(((bf16[256,144]{0,1:T(8,128)(2,1)}), bf16[256,2304]{0,1:T(8,128)(2,1)}) %all-gather.11.cloned.1.call-update) | async-done | bytes 1179664 | tf_op jit(solution)/shard_map/all_gather | solution.py:52
  135.2 1.5 fusion.88
  136.7 4.9 gather_fusion.9
  141.9 2.6 gather_fusion.7
  144.5 2.6 gather_fusion.5
  147.1 2.6 gather_fusion.3
  149.6 2.6 gather_fusion.1
  152.2 1.6 copy.26
  153.8 2.2 gather_fusion.6
  155.9 2.0 gather_fusion.4
  157.9 2.1 gather_fusion.2
  160.0 2.2 gather_fusion
  162.2 0.7 mul.148
  163.0 0.7 mul.143
  163.6 0.7 mul.133
  164.3 0.7 mul.138
  165.0 124.3 %all-gather.13.cloned.1.call-done = bf16[4,2,2304,360]{3,2,0,1:T(8,128)(2,1)} async-done(((bf16[4,2,144,360]{3,2,0,1:T(8,128)(2,1)}), bf16[4,2,2304,360]{3,2,0,1:T(8,128)(2,1)}) %all-gather.13.cloned.1.call-update) | async-done | bytes 13271056 | tf_op jit(solution)/shard_map/all_gather | solution.py:58
  289.3 2.3 fusion.7
  291.5 93.7 %all-gather.15.cloned.1.call-done = bf16[4,360,2304]{1,2,0:T(8,128)(2,1)} async-done(((bf16[4,360,144]{1,2,0:T(8,128)(2,1)}), bf16[4,360,2304]{1,2,0:T(8,128)(2,1)}) %all-gather.15.cloned.1.call-update) | async-done | bytes 6635536 | tf_op jit(solution)/shard_map/all_gather | solution.py:62
  385.3 4.4 convolution_multiply_fusion.3
  389.7 5.1 scatter_custom_fusion.3
  394.7 2.0 fusion.5
  396.8 4.4 convolution_multiply_fusion.2
  401.1 6.6 scatter_fusion
  407.7 2.0 fusion.3
  409.7 4.4 convolution_multiply_fusion.1
  414.1 6.6 scatter_fusion.1
  420.7 2.0 fusion.1
  422.7 4.4 convolution_multiply_fusion
  427.1 6.5 scatter_fusion.2
  433.6 1.8 convert_element_type.97
  435.4 1.4 copy.37
  436.8 1.0 copy.32
  438.1 81.9 %reduce-scatter.4.cloned.1.call-done = bf16[144,256]{1,0:T(8,128)(2,1)} async-done(((bf16[2304,256]{1,0:T(8,128)(2,1)}), bf16[144,256]{1,0:T(8,128)(2,1)}) %reduce-scatter.4.cloned.1.call-update) | async-done | bytes 73744
  520.0 1.0 copy.38
  521.0 0.8 copy.36
  521.8 0.6 gather_fusion.8
  522.4 37.8 %all-gather.3 = f32[16,144,4]{1,2,0:T(4,128)S(1)} all-gather(f32[1,144,4]{1,2,0:T(4,128)S(1)} %bitcast.148), channel_id=2, replica_groups=mesh['dp'=16,'mp'=16] {'mp'}, dimensions={0}, use_global_device_ids=true | all-gather | bytes 39168 | tf_op jit(solution)/shard_map/all_gather | solution.py:80
  560.5 30.4 %all-gather.4 = bf16[16,4,2304]{2,1,0:T(4,128)(2,1)S(1)} all-gather(bf16[1,4,2304]{2,1,0:T(4,128)(2,1)S(1)} %fusion.42), channel_id=1, replica_groups=mesh['dp'=16,'mp'=16] {'dp'}, dimensions={0}, use_global_device_ids=true | all-gather | bytes 313344 | tf_op jit(solution)/shard_map/all_gather | solution.py:85
  591.0 0.6 fusion.87
  591.8 36.8 %all-gather.5 = f32[16,2,64]{2,1,0:T(2,128)S(1)} all-gather(f32[1,2,64]{2,1,0:T(2,128)S(1)} %maximum_bitcast_fusion), channel_id=3, replica_groups=mesh['dp'=16,'mp'=16] {'mp'}, dimensions={0}, use_global_device_ids=true | all-gather | bytes 8704 | tf_op jit(solution)/shard_map/all_gather | solution.py:93
  628.7 24.0 %all-gather.6 = f32[16,2,64]{2,1,0:T(2,128)S(1)} all-gather(f32[1,2,64]{2,1,0:T(2,128)S(1)} %maximum_bitcast_fusion.1), channel_id=4, replica_groups=mesh['dp'=16,'mp'=16] {'dp'}, dimensions={0}, use_global_device_ids=true | all-gather | bytes 8704 | tf_op jit(solution)/shard_map/all_gather | solution.py:93
  652.7 0.8 subtract_subtract_fusion
  (96 shorter events, 4.1 us)
Async XLA Ops:
  7.2 583.8 %copy-start = (bf16[2304,512]{1,0:T(8,128)(2,1)S(1)}, bf16[2304,512]{1,0:T(8,128)(2,1)}, u32[]{:S(2)}) copy-start(bf16[2304,512]{1,0:T(8,128)(2,1)} %param.20) | copy-start | bytes 7077892
  7.2 50.7 %copy-start.5 = (s32[256,2]{0,1:T(2,128)S(1)}, s32[256,2]{0,1:T(2,128)}, u32[]{:S(2)}) copy-start(s32[256,2]{0,1:T(2,128)} %param.12) | copy-start | bytes 6148
  7.2 128.0 %all-gather.11.cloned.1.call-start = ((), (), s32[]{:S(2)}) async-start(), calls=%async_computation.1 | async-start | bytes 1253376 | tf_op jit(solution)/shard_map/all_gather | solution.py:52
  54.8 234.5 %all-gather.13.cloned.1.call-start = ((), (), s32[]{:S(2)}) async-start(), calls=%async_computation.2 | async-start | bytes 15040512 | tf_op jit(solution)/shard_map/all_gather | solution.py:58
  54.8 80.4 %copy-start.6 = (bf16[2304,4]{0,1:T(4,128)(2,1)S(1)}, bf16[2304,4]{0,1:T(4,128)(2,1)}, u32[]{:S(2)}) copy-start(bf16[2304,4]{0,1:T(4,128)(2,1)} %param.15) | copy-start | bytes 55300
  57.1 328.2 %all-gather.15.cloned.1.call-start = ((), (), s32[]{:S(2)}) async-start(), calls=%async_computation.3 | async-start | bytes 7520256 | tf_op jit(solution)/shard_map/all_gather | solution.py:62
  57.9 462.1 %reduce-scatter.4.cloned.1.call-start = ((), (), s32[]{:S(2)}) async-start(), calls=%async_computation.4 | async-start | bytes 1253376
  81.2 0.6 copy-start.9
  160.0 4.3 copy-start.8
  162.2 223.1 %copy-start.4 = (bf16[160,2304]{1,0:T(8,128)(2,1)S(1)}, bf16[160,2304]{1,0:T(8,128)(2,1)}, u32[]{:S(2)}) copy-start(bf16[160,2304]{1,0:T(8,128)(2,1)} %gather_fusion) | copy-start | bytes 2211844
  389.7 5.1 copy-start.3
  401.1 6.6 copy-start.2
  414.1 6.6 copy-start.1
  435.4 2.5 copy-start.10
  435.4 2.7 copy-start.11
  436.8 123.6 %copy-start.7 = (f32[2304]{0:T(1024)S(1)}, f32[2304]{0:T(1024)}, u32[]{:S(2)}) copy-start(f32[2304]{0:T(1024)} %param.19) | copy-start | bytes 27652
Sparse Core Ops, SparseCore 0:
  54.9 80.2 all-gather.10
  137.9 151.3 all-gather.12
  292.0 93.2 all-gather.14
  437.0 82.9 reduce-scatter.3

commit v3 on v2

--- a/solution.py
+++ b/solution.py
@@ -55,29 +55,40 @@
     tables = [slot_tables(chosen_specialists, expert, CAP) for expert in range(experts)]
     inputs = jnp.stack([features[table[0]] for table in tables])
     scales = jnp.stack([mixing[table[0], table[2]] * table[1] for table in tables])
-    pair_weights = lax.all_gather(
-        jnp.stack([specialist_switch_weights, specialist_expand_weights], axis=1),
+    all_weights = lax.all_gather(
+        jnp.stack(
+            [
+                specialist_switch_weights,
+                specialist_expand_weights,
+                jnp.swapaxes(specialist_contract_weights, 1, 2),
+            ],
+            axis=1,
+        ),
         "dp", axis=2, tiled=True,
     )
-    down_weights = lax.all_gather(specialist_contract_weights, "dp", axis=2, tiled=True)
     pieces_out = []
     for expert in range(experts):
         rows_in = inputs[expert]
-        gate = jnp.dot(rows_in, pair_weights[expert, 0], preferred_element_type=jnp.float32)
-        up_part = jnp.dot(rows_in, pair_weights[expert, 1], preferred_element_type=jnp.float32)
+        gate = jnp.dot(rows_in, all_weights[expert, 0], preferred_element_type=jnp.float32)
+        up_part = jnp.dot(rows_in, all_weights[expert, 1], preferred_element_type=jnp.float32)
         act = (jax.nn.silu(gate) * up_part).astype(jnp.bfloat16)
-        pieces_out.append(jnp.dot(act, down_weights[expert], preferred_element_type=jnp.float32))
+        pieces_out.append(
+            lax.dot_general(
+                act, all_weights[expert, 2], (((1,), (1,)), ((), ())),
+                preferred_element_type=jnp.float32,
+            )
+        )
     outputs = jnp.stack(pieces_out)
     combined = jnp.zeros((tok_rows, EMBED_DIMENSION), jnp.float32)
     for expert in range(experts):
         combined = combined.at[tables[expert][0]].add(outputs[expert] * scales[expert][:, None])
-    branch = lax.psum_scatter(
-        combined.astype(jnp.bfloat16), "mp", scatter_dimension=1, tiled=True
-    ).astype(jnp.float32)
+    ends_index = jnp.cumsum(sequence_piece_tallies[0], dtype=jnp.int32) - 1
+    partial_rows = combined.astype(jnp.bfloat16)
+    branch = lax.psum_scatter(partial_rows, "mp", scatter_dimension=1, tiled=True).astype(jnp.float32)
     new_hidden = skip_stream_arriving + branch_scale * branch
-    ends_index = jnp.cumsum(sequence_piece_tallies[0], dtype=jnp.int32) - 1
-    end_local = new_hidden[ends_index]
-    end_rows = lax.all_gather(end_local, "mp", axis=1, tiled=True)
+    skip_ends = lax.all_gather(skip_stream_arriving[ends_index], "mp", axis=1, tiled=True)
+    end_partials = lax.all_gather(partial_rows[ends_index], "mp", axis=0)
+    end_rows = skip_ends + branch_scale * jnp.sum(end_partials.astype(jnp.float32), axis=0)
     end_squares = jnp.sum(end_rows * end_rows, axis=1)
     end_normed = (
         end_rows * lax.rsqrt(end_squares / EMBED_DIMENSION + epsilon)[:, None] * terminal_rmsnorm_gain

time: 664 us -> 551 us (0.83)
  waiting for transfers between devices: 354 us -> 195 us
  blocking collectives: 174 us -> 217 us
    all_gather x1 -> x0, waiting for transfers between devices: 93.7 us -> none  [body(): lax.all_gather(specialist_contract_weights, 'dp', axis=2, tiled=True)]
    unnamed x5 -> x4, waiting for transfers between devices: 82.6 us -> 0.05 us
    all_gather x1, waiting for transfers between devices: 124 us -> 181 us  [body(): lax.all_gather(jnp.stack([specialist_switch_weights, specialist_expand_we...]
    all_gather x1 -> x2, blocking collectives: 37.8 us -> 77.6 us  [the longest x1 40.1 us: body(): end_partials = lax.all_gather(partial_rows[ends_index], 'mp', axis=0)]
    all_gather x1, waiting for transfers between devices: 53.4 us -> 14 us  [body(): features = lax.all_gather(normed_local, 'mp', axis=1, tiled=True)]
  transfers between devices with their start and end apart: 4 -> 3, of which waited for: 4 -> 2; matrix products, arithmetic and copies ran while one was open for 9% -> 11% of each run, Pallas kernels for 0% -> 0%
where the time goes in v3:
time: 551 us; the launch traced here: 547 us
  blocking collectives  217 us (39%)
  waiting for transfers between devices  195 us (35%)
  local copies, waits for them, and re-layouts  51.4 us (9%)
  other arithmetic  41.2 us (7%)
  matrix products  27.9 us (5%)
  between operations  14.1 us (3%)
    all_gather x1, waiting for transfers between devices, body(): lax.all_gather(jnp.stack([specialist_switch_weights, specialist_expand_we...  181 us
    all_gather x2, blocking collectives, body(): held = lax.all_gather(stats, axis, axis=0)  67.2 us
    psum x1, blocking collectives, body(): lax.psum(jnp.sum(skip_stream_arriving * skip_stream_arriving, axis=1), 'mp')  44.8 us
    all_gather x1, blocking collectives, body(): end_partials = lax.all_gather(partial_rows[ends_index], 'mp', axis=0)  40.1 us
    all_gather x1, blocking collectives, body(): lax.all_gather(skip_stream_arriving[ends_index], 'mp', axis=1, tiled=True)  37.5 us
    all_gather x1, blocking collectives, body(): lax.all_gather(end_normed, 'dp', axis=0, tiled=True)  27.8 us
    scatter-add x4, other arithmetic, body(): combined.at[tables[expert][0]]  24.8 us
    dot_general x4, matrix products, body(): lax.dot_general(act, all_weights[expert, 2], (((1,), (1,)), ((), ())), pr...  17.4 us
  transfers between devices with their start and end apart: 3, of which 2 were waited for; matrix products, arithmetic and copies ran while one was open for 11% of the time, Pallas kernels for 0%

profile of v3, /device:TPU:8, one launch (start us, length us, event | category | flops | bytes accessed | tf_op | source)
XLA Modules:
  0.0 546.8 jit_solution(18091905649813592468)
XLA Ops:
  7.2 1.1 multiply_reduce_fusion
  8.3 44.8 %psum.7 = f32[256]{0:T(256)S(1)} all-reduce(f32[256]{0:T(256)S(1)} %multiply_reduce_fusion), channel_id=1, replica_groups=mesh['dp'=16,'mp'=16] {'mp'}, use_global_device_ids=true, to_apply=%region_5.6 | all-reduce | flops 256 | bytes 2048 | tf_op jit(solution)/shard_map/psum | solution.py:46
  53.1 1.6 multiply_convert_fusion
  54.9 2.7 pad_maximum_fusion
  59.7 1.4 scatter_custom_fusion
  61.1 2.0 scatter_custom_fusion.2
  63.1 1.9 scatter_custom_fusion.6
  65.0 1.4 scatter_custom_fusion.4
  67.2 1.9 scatter_custom_fusion.10
  69.2 1.4 scatter_custom_fusion.8
  70.6 2.0 scatter_custom_fusion.14
  72.5 1.4 scatter_custom_fusion.12
  73.9 1.4 scatter_custom_fusion.9
  75.4 1.4 scatter_custom_fusion.5
  76.8 1.6 scatter_custom_fusion.13
  78.3 1.4 scatter_custom_fusion.1
  80.1 0.6 gather_fusion.8
  80.6 37.5 %all-gather.4 = f32[16,144,4]{1,2,0:T(4,128)S(1)} all-gather(f32[1,144,4]{1,2,0:T(4,128)S(1)} %bitcast.158), channel_id=2, replica_groups=mesh['dp'=16,'mp'=16] {'mp'}, dimensions={0}, use_global_device_ids=true | all-gather | bytes 39168 | tf_op jit(solution)/shard_map/all_gather | solution.py:89
  118.1 0.7 reshape.574
  118.8 0.6 pad_clamp_fusion.2
  119.4 0.6 pad_clamp_fusion.3
  120.0 0.6 pad_clamp_fusion.1
  120.7 0.6 pad_clamp_fusion.4
  121.3 0.6 broadcast_multiply_fusion
  121.8 14.0 %all-gather.12.cloned.1.call-done = bf16[256,2304]{0,1:T(8,128)(2,1)} async-done(((bf16[256,144]{0,1:T(8,128)(2,1)}), bf16[256,2304]{0,1:T(8,128)(2,1)}) %all-gather.12.cloned.1.call-update) | async-done | bytes 1179664 | tf_op jit(solution)/shard_map/all_gather | solution.py:52
  135.8 1.5 fusion.88
  137.4 4.9 gather_fusion.10
  142.6 2.6 gather_fusion.7
  145.1 2.5 gather_fusion.5
  147.7 2.6 gather_fusion.3
  150.2 2.6 gather_fusion.1
  152.8 1.6 copy.28
  154.4 2.1 gather_fusion.6
  156.5 2.1 gather_fusion.4
  158.7 2.1 gather_fusion.2
  160.7 2.1 gather_fusion
  162.8 0.8 mul.154
  163.6 0.7 mul.149
  164.3 0.7 mul.139
  164.9 0.7 mul.144
  165.6 180.5 %all-gather.14.cloned.1.call-done = bf16[4,3,2304,360]{3,2,0,1:T(8,128)(2,1)} async-done(((bf16[4,3,144,360]{3,2,0,1:T(8,128)(2,1)}), bf16[4,3,2304,360]{3,2,0,1:T(8,128)(2,1)}) %all-gather.14.cloned.1.call-update) | async-done | bytes 19906576 | tf_op jit(solution)/shard_map/all_gather | solution.py:58
  346.2 2.3 fusion.7
  348.4 4.4 convolution_multiply_fusion.3
  352.8 5.1 scatter_custom_fusion.3
  357.9 2.0 fusion.5
  359.9 4.4 convolution_multiply_fusion.2
  364.2 6.6 %scatter_fusion = f32[256,2304]{1,0:T(8,128)} fusion(f32[256,2304]{1,0:T(8,128)} %scatter_custom_fusion.3, s32[160]{0:T(256)S(1)} %get-tuple-element.29, f32[160,2304]{1,0:T(8,128)} %convolution_multiply_fusion.2), kind=kCustom, calls=%fused_computation.18 | custom fusion | flops 368640 | bytes 4424320 | tf_op jit(solution)/shard_map/scatter-add | solution.py:84
  370.8 2.0 fusion.3
  372.9 4.4 convolution_multiply_fusion.1
  377.2 6.6 %scatter_fusion.1 = f32[256,2304]{1,0:T(8,128)} fusion(f32[256,2304]{1,0:T(8,128)} %scatter_fusion, s32[160]{0:T(256)S(1)} %get-tuple-element.27, f32[160,2304]{1,0:T(8,128)} %convolution_multiply_fusion.1), kind=kCustom, calls=%fused_computation.22 | custom fusion | flops 368640 | bytes 4424320 | tf_op jit(solution)/shard_map/scatter-add | solution.py:84
  383.8 2.0 fusion.1
  385.8 4.4 convolution_multiply_fusion
  390.2 6.5 %scatter_fusion.2 = f32[256,2304]{1,0:T(8,128)} fusion(f32[256,2304]{1,0:T(8,128)} %scatter_fusion.1, s32[160]{0:T(256)S(1)} %get-tuple-element.25, f32[160,2304]{1,0:T(8,128)} %convolution_multiply_fusion), kind=kCustom, calls=%fused_computation.26 | custom fusion | flops 368640 | bytes 4424320 | tf_op jit(solution)/shard_map/scatter-add | solution.py:84
  396.7 1.8 convert_element_type.100
  398.5 1.2 gather_fusion.9
  399.7 1.4 copy.40
  401.1 40.1 %all-gather.5 = bf16[16,4,2304]{2,1,0:T(4,128)(2,1)S(1)} all-gather(bf16[1,4,2304]{2,1,0:T(4,128)(2,1)} %bitcast.153), channel_id=3, replica_groups=mesh['dp'=16,'mp'=16] {'mp'}, dimensions={0}, use_global_device_ids=true | all-gather | bytes 313344 | tf_op jit(solution)/shard_map/all_gather | solution.py:90
  441.6 27.8 %all-gather.6 = bf16[16,4,2304]{2,1,0:T(4,128)(2,1)S(1)} all-gather(bf16[1,4,2304]{2,1,0:T(4,128)(2,1)S(1)} %fusion.42), channel_id=1, replica_groups=mesh['dp'=16,'mp'=16] {'dp'}, dimensions={0}, use_global_device_ids=true | all-gather | bytes 313344 | tf_op jit(solution)/shard_map/all_gather | solution.py:96
  469.5 0.6 fusion.87
  470.3 37.3 %all-gather.7 = f32[16,2,64]{2,1,0:T(2,128)S(1)} all-gather(f32[1,2,64]{2,1,0:T(2,128)S(1)} %maximum_bitcast_fusion), channel_id=4, replica_groups=mesh['dp'=16,'mp'=16] {'mp'}, dimensions={0}, use_global_device_ids=true | all-gather | bytes 8704 | tf_op jit(solution)/shard_map/all_gather | solution.py:104
  507.7 29.9 %all-gather.8 = f32[16,2,64]{2,1,0:T(2,128)S(1)} all-gather(f32[1,2,64]{2,1,0:T(2,128)S(1)} %maximum_bitcast_fusion.1), channel_id=5, replica_groups=mesh['dp'=16,'mp'=16] {'dp'}, dimensions={0}, use_global_device_ids=true | all-gather | bytes 8704 | tf_op jit(solution)/shard_map/all_gather | solution.py:104
  537.7 0.8 subtract_subtract_fusion
  538.4 1.0 copy.41
  539.5 0.8 copy.39
  (104 shorter events, 4.5 us)
Async XLA Ops:
  7.2 462.3 %copy-start = (bf16[2304,512]{1,0:T(8,128)(2,1)S(1)}, bf16[2304,512]{1,0:T(8,128)(2,1)}, u32[]{:S(2)}) copy-start(bf16[2304,512]{1,0:T(8,128)(2,1)} %param.20) | copy-start | bytes 7077892
  7.2 128.7 %all-gather.12.cloned.1.call-start = ((), (), s32[]{:S(2)}) async-start(), calls=%async_computation.1 | async-start | bytes 1253376 | tf_op jit(solution)/shard_map/all_gather | solution.py:52
  54.8 291.4 %all-gather.14.cloned.1.call-start = ((), (), s32[]{:S(2)}) async-start(), calls=%async_computation.2 | async-start | bytes 22560768 | tf_op jit(solution)/shard_map/all_gather | solution.py:58
  54.8 2.8 copy-start.1
  54.8 3.0 copy-start.14
  54.9 3.2 copy-start.9
  57.6 63.7 %copy-start.15 = (f32[64]{0:T(128)S(1)}, f32[64]{0:T(128)}, u32[]{:S(2)}) copy-start(f32[64]{0:T(128)} %param.21) | copy-start | bytes 772
  57.6 78.3 %copy-start.10 = (bf16[2304,4]{0,1:T(4,128)(2,1)S(1)}, bf16[2304,4]{0,1:T(4,128)(2,1)}, u32[]{:S(2)}) copy-start(bf16[2304,4]{0,1:T(4,128)(2,1)} %param.15) | copy-start | bytes 55300
  57.6 480.8 %reduce-scatter.4.cloned.1.call-start = ((), (), s32[]{:S(2)}) async-start(), calls=%async_computation.3 | async-start | bytes 1253376
  57.8 84.4 %copy-start.2 = (f32[256,144]{1,0:T(8,128)}, f32[256,144]{1,0:T(8,128)S(1)}, u32[]{:S(2)}) copy-start(f32[256,144]{1,0:T(8,128)S(1)} %copy.34) | copy-start | bytes 442372
  120.7 16.7 %copy-start.12 = (s32[160]{0:T(256)}, s32[160]{0:T(256)S(1)}, u32[]{:S(2)}) copy-start(s32[160]{0:T(256)S(1)} %get-tuple-element.31) | copy-start | bytes 1924
  162.8 185.6 %copy-start.7 = (bf16[160,2304]{1,0:T(8,128)(2,1)S(1)}, bf16[160,2304]{1,0:T(8,128)(2,1)}, u32[]{:S(2)}) copy-start(bf16[160,2304]{1,0:T(8,128)(2,1)} %gather_fusion) | copy-start | bytes 2211844
  352.8 5.1 copy-start.6
  364.2 6.6 %copy-start.5 = (bf16[160,2304]{1,0:T(8,128)(2,1)S(1)}, bf16[160,2304]{1,0:T(8,128)(2,1)}, u32[]{:S(2)}) copy-start(bf16[160,2304]{1,0:T(8,128)(2,1)} %gather_fusion.4) | copy-start | bytes 2211844
  377.2 6.6 %copy-start.4 = (bf16[160,2304]{1,0:T(8,128)(2,1)S(1)}, bf16[160,2304]{1,0:T(8,128)(2,1)}, u32[]{:S(2)}) copy-start(bf16[160,2304]{1,0:T(8,128)(2,1)} %gather_fusion.6) | copy-start | bytes 2211844
  399.7 41.8 %copy-start.11 = (f32[2304]{0:T(1024)S(1)}, f32[2304]{0:T(1024)}, u32[]{:S(2)}) copy-start(f32[2304]{0:T(1024)} %param.19) | copy-start | bytes 27652
  401.1 40.3 %copy-start.8 = (f32[2304,4]{0,1:T(4,128)S(1)}, f32[2304,4]{0,1:T(4,128)}, u32[]{:S(2)}) copy-start(f32[2304,4]{0,1:T(4,128)} %reshape.574) | copy-start | bytes 110596
  401.1 68.4 %copy-start.13 = (f32[64]{0:T(128)S(1)}, f32[64]{0:T(128)}, u32[]{:S(2)}) copy-start(f32[64]{0:T(128)} %broadcast_multiply_fusion) | copy-start | bytes 772
  469.5 69.9 %copy-start.3 = (f32[256,144]{1,0:T(8,128)S(1)}, f32[256,144]{1,0:T(8,128)}, u32[]{:S(2)}) copy-start(f32[256,144]{1,0:T(8,128)} %copy-done.2) | copy-start | bytes 442372
Sparse Core Ops, SparseCore 0:
  54.9 80.8 all-gather.11
  138.5 207.5 all-gather.13
  401.2 84.0 reduce-scatter.3
